TPU v7x, 512 devices: a whole 4x8x8 slice. The times are simulated.
512 devices in a mesh: row: 8 (over z_lo, core), col: 8 (over x, z_hi), tm: 8 (over y).
Axes of the slice: x: 4, y: 8, z: 8 (z_hi: 2, z_lo: 4; z = z_hi * 4 + z_lo), core: 2. Of those that a mesh axis runs over, the one named last changes fastest.
Arguments:
- green_occ: bfloat16 [16, 256, 30720], P('tm', 'row', 'col'), may hold values from -6 to 6
- green_virt: bfloat16 [16, 256, 30720], P('tm', 'row', 'col'), may hold values from -6 to 6
- adjoint_w: bfloat16 [16, 256, 30720], P(None, 'row', ('col', 'tm')), may hold values from -6 to 6
- grad_basis: float32 [3, 256], P(None, 'row'), may hold values from -6 to 6
- owner_map: int32 [30720], replicated, may hold values from 0 to 999
- block_offset: int32 [8], P('row'), may hold values from 0 to 30688
Outputs:
- chi_freq: bfloat16 [16, 256, 30720], P(None, 'row', ('col', 'tm'))
- forces: float32 [3, 1000], replicated
All inputs are finite; a program needn't handle non-finite values.
Results may differ from a plain program's by a relative error of at most 0.0085.
Values may be sent and summed in bfloat16 or wider, within the bound.
No kernel may reach another device: no remote copies, remote signals or barrier semaphores. Data moves between devices by JAX's collectives and lax.ppermute only.
A program may use at most 64 MiB of HBM per device.

v0:
```python
import math
import jax
import jax.numpy as jnp
from jax import lax
from jax.sharding import PartitionSpec as P

NG = 30720
NTAU = 16
NATOM = 1000


def cos_table(count):
    steps = jnp.arange(count).astype(jnp.float32)
    tau = 0.1 * jnp.power(jnp.float32(1.35), steps)
    omega = 0.15 * jnp.power(jnp.float32(1.35), steps)
    return jnp.cos(omega[:, None] * tau[None, :]) / 4.0


def on_device(green_occ, green_virt, adjoint_w, grad_basis, owner_map, block_offset):
    table = cos_table(NTAU)
    scale = 1.0 / math.sqrt(NTAU * NG)
    row_count = green_occ.shape[1]
    product = (green_occ.astype(jnp.float32) * green_virt.astype(jnp.float32)).astype(jnp.bfloat16)
    chi_freq = jnp.einsum(
        "kt,tnc->knc",
        table,
        lax.all_to_all(product, "tm", split_axis=2, concat_axis=0, tiled=True).astype(jnp.float32),
        precision=lax.Precision.HIGHEST,
    ).astype(jnp.bfloat16)
    partial_value = (
        jnp.sum(adjoint_w.astype(jnp.float32) * chi_freq.astype(jnp.float32), axis=(0, 2)) * scale
    )
    owners = lax.dynamic_slice_in_dim(owner_map, block_offset[0], row_count, 0)
    onehot = (owners[:, None] == jnp.arange(NATOM)[None, :]).astype(jnp.float32)
    energy = lax.psum(partial_value, ("col", "tm"))
    local_forces = jnp.dot(
        grad_basis * energy[None, :],
        onehot,
        precision=lax.Precision.HIGHEST,
        preferred_element_type=jnp.float32,
    )
    forces = lax.psum(local_forces, "row")
    return (chi_freq, forces)


def solution(mesh):
    in_specs = (
        P("tm", "row", "col"),
        P("tm", "row", "col"),
        P(None, "row", ("col", "tm")),
        P(None, "row"),
        P(),
        P("row"),
    )
    out_specs = (P(None, "row", ("col", "tm")), P())
    return jax.shard_map(
        on_device, mesh=mesh, in_specs=in_specs, out_specs=out_specs, check_vma=False
    )
```

profile of v0, /device:TPU:1, one launch (start us, length us, event | category | flops | bytes accessed | tf_op | source)
XLA Modules:
  0.0 282.4 jit_solution(8296169190990714850)
XLA Ops:
  0.6 1.3 multiply_convert_fusion
  1.9 1.4 copy.16
  3.3 2.5 reshape.19
  5.9 7.7 %all-to-all-start = ((bf16[8,2,15360]{2,1,0:T(2,128)(2,1)}), bf16[8,2,15360]{2,1,0:T(2,128)(2,1)S(1)}, u32[]{:S(2)}, u32[]{:S(2)}) async-start(bf16[8,2,15360]{2,1,0:T(2,128)(2,1)} %reshape.19), calls=%async_computation | async-start | bytes 983040 | tf_op jit(solution)/shard_map/all_to_all | solution.py:27
  14.2 0.8 dynamic_slice.3
  15.0 12.4 %all-to-all-done = bf16[8,2,15360]{2,1,0:T(2,128)(2,1)S(1)} async-done(((bf16[8,2,15360]{2,1,0:T(2,128)(2,1)}), bf16[8,2,15360]{2,1,0:T(2,128)(2,1)S(1)}, u32[]{:S(2)}, u32[]{:S(2)}) %all-to-all-start) | async-done | bytes 491552 | tf_op jit(solution)/shard_map/all_to_all | solution.py:27
  27.4 1.0 reshape.20
  28.4 0.0 copy-start
  28.4 1.5 copy.17
  29.9 0.0 copy-start.1
  29.9 0.4 all_to_all.16
  30.3 0.0 copy-done
  30.4 1.1 multiply_reduce_fusion
  31.5 1.1 copy.19
  32.5 196.4 %psum.14 = f32[32]{0:T(128)S(1)} all-reduce(f32[32]{0:T(128)S(1)} %broadcast_multiply_fusion), channel_id=1, replica_groups=mesh['row'=8,'col'=8,'tm'=8] {'col','tm'}, use_global_device_ids=true, to_apply=%region_1.0 | all-reduce | flops 32 | bytes 256 | tf_op jit(solution)/shard_map/psum | solution.py:35
  228.9 0.0 copy-done.1
  228.9 0.2 fusion
  229.1 53.3 %psum.15 = f32[3,1000]{1,0:T(4,128)} all-reduce(f32[3,1000]{1,0:T(4,128)S(1)} %fusion), channel_id=1, replica_groups=mesh['row'=8,'col'=8,'tm'=8] {'row'}, use_global_device_ids=true, to_apply=%region_2.0 | all-reduce | flops 3000 | bytes 24000 | tf_op jit(solution)/shard_map/psum | solution.py:42
  (2 shorter events, 0.0 us)
Async XLA Ops:
  5.9 21.5 %all-to-all-start = ((bf16[8,2,15360]{2,1,0:T(2,128)(2,1)}), bf16[8,2,15360]{2,1,0:T(2,128)(2,1)S(1)}, u32[]{:S(2)}, u32[]{:S(2)}) async-start(bf16[8,2,15360]{2,1,0:T(2,128)(2,1)} %reshape.19), calls=%async_computation | async-start | bytes 983040 | tf_op jit(solution)/shard_map/all_to_all | solution.py:27
  28.4 2.0 copy-start
  29.9 199.0 %copy-start.1 = (f32[3,32]{1,0:T(4,128)S(1)}, f32[3,32]{1,0:T(4,128)}, u32[]{:S(2)}) copy-start(f32[3,32]{1,0:T(4,128)} %param.9) | copy-start | bytes 1156
where the time goes:
time: 283 us; the launch traced here: 282 us
  blocking collectives  250 us (88%)
  waiting for transfers between devices  12.4 us (4%)
  local copies, waits for them, and re-layouts  8.71 us (3%)
  starting transfers between devices  7.65 us (3%)
    psum x1, blocking collectives, on_device(): energy = lax.psum(partial_value, ('col', 'tm'))  196 us
    psum x1, blocking collectives, on_device(): forces = lax.psum(local_forces, 'row')  53.3 us
    all_to_all x1, waiting for transfers between devices, on_device(): lax.all_to_all(product, 'tm', split_axis=2, concat_axis=0, tiled=True)  12.4 us
    all_to_all x1, starting transfers between devices, on_device(): lax.all_to_all(product, 'tm', split_axis=2, concat_axis=0, tiled=True)  7.65 us
  transfers between devices with their start and end apart: 1, of which 1 were waited for; matrix products, arithmetic and copies ran while one was open for 0% of the time, Pallas kernels for 0%

commit v1 on v0

--- a/solution.py
+++ b/solution.py
@@ -32,7 +32,7 @@
     )
     owners = lax.dynamic_slice_in_dim(owner_map, block_offset[0], row_count, 0)
     onehot = (owners[:, None] == jnp.arange(NATOM)[None, :]).astype(jnp.float32)
-    energy = lax.psum(partial_value, ("col", "tm"))
+    energy = lax.psum(lax.psum(partial_value, "tm"), "col")
     local_forces = jnp.dot(
         grad_basis * energy[None, :],
         onehot,

time: 283 us -> 112 us (0.40)
  the two profiles are of different devices: /device:TPU:1 before, /device:TPU:8 now
where the time goes in v1:
time: 112 us; the launch traced here: 111 us
  blocking collectives  77.1 us (69%)
  waiting for transfers between devices  12.2 us (11%)
  starting transfers between devices  9.21 us (8%)
  local copies, waits for them, and re-layouts  8.71 us (8%)
  between operations  1.36 us (1%)
  matrix products  1.31 us (1%)
  other arithmetic  1.3 us (1%)
    psum x2, blocking collectives, on_device(): energy = lax.psum(lax.psum(partial_value, 'tm'), 'col')  50.6 us
    psum x1, blocking collectives, on_device(): forces = lax.psum(local_forces, 'row')  26.5 us
    all_to_all x1, waiting for transfers between devices, on_device(): lax.all_to_all(product, 'tm', split_axis=2, concat_axis=0, tiled=True)  12.2 us
    all_to_all x1, starting transfers between devices, on_device(): lax.all_to_all(product, 'tm', split_axis=2, concat_axis=0, tiled=True)  9.21 us
    unnamed x7, local copies, waits for them, and re-layouts  4.61 us
  transfers between devices with their start and end apart: 1, of which 1 were waited for; matrix products, arithmetic and copies ran while one was open for 1% of the time, Pallas kernels for 0%

profile of v1, /device:TPU:8, one launch (start us, length us, event | category | flops | bytes accessed | tf_op | source)
XLA Modules:
  0.0 111.2 jit_solution(13592653235829732455)
XLA Ops:
  0.6 1.3 %multiply_convert_fusion = bf16[2,32,3840]{2,1,0:T(8,128)(2,1)S(1)} fusion(bf16[2,32,3840]{2,1,0:T(8,128)(2,1)} %param.7, bf16[2,32,3840]{2,1,0:T(8,128)(2,1)} %param.6), kind=kLoop, calls=%fused_computation.2 | loop fusion | flops 983040 | bytes 1474560 | tf_op jit(solution)/shard_map/convert_element_type | solution.py:23
  1.9 1.4 %copy.16 = bf16[2,32,3840]{1,0,2:T(2,128)(2,1)S(1)} copy(bf16[2,32,3840]{2,1,0:T(8,128)(2,1)S(1)} %multiply_convert_fusion) | data formatting | bytes 983040 | tf_op jit(solution)/shard_map/convert_element_type | solution.py:23
  3.3 2.5 %reshape.19 = bf16[8,2,15360]{2,1,0:T(2,128)(2,1)} reshape(bf16[3840,2,32]{2,1,0:T(2,128)(2,1)S(1)} %bitcast.16) | data formatting | bytes 983040
  5.9 9.2 %all-to-all-start = ((bf16[8,2,15360]{2,1,0:T(2,128)(2,1)}), bf16[8,2,15360]{2,1,0:T(2,128)(2,1)S(1)}, u32[]{:S(2)}, u32[]{:S(2)}) async-start(bf16[8,2,15360]{2,1,0:T(2,128)(2,1)} %reshape.19), calls=%async_computation | async-start | bytes 983040 | tf_op jit(solution)/shard_map/all_to_all | solution.py:27
  15.7 0.8 dynamic_slice.3
  16.5 12.2 %all-to-all-done = bf16[8,2,15360]{2,1,0:T(2,128)(2,1)S(1)} async-done(((bf16[8,2,15360]{2,1,0:T(2,128)(2,1)}), bf16[8,2,15360]{2,1,0:T(2,128)(2,1)S(1)}, u32[]{:S(2)}, u32[]{:S(2)}) %all-to-all-start) | async-done | bytes 491552 | tf_op jit(solution)/shard_map/all_to_all | solution.py:27
  28.8 1.0 reshape.20
  29.7 0.0 copy-start
  29.7 1.5 %copy.17 = bf16[2,32,8,480]{3,0,2,1:T(2,128)(2,1)S(1)} copy(bf16[2,32,8,480]{1,0,3,2:T(2,128)(2,1)S(1)} %bitcast.17) | data formatting | bytes 983040 | tf_op jit(solution)/shard_map/all_to_all | solution.py:27
  31.3 0.0 copy-start.1
  31.3 0.4 all_to_all.16
  31.7 0.0 copy-done
  31.7 1.1 multiply_reduce_fusion
  32.8 1.1 copy.19
  33.9 15.6 %psum.21 = f32[32]{0:T(128)S(1)} all-reduce(f32[32]{0:T(128)S(1)} %broadcast_multiply_fusion), channel_id=1, replica_groups=mesh['row'=8,'col'=8,'tm'=8] {'tm'}, use_global_device_ids=true, to_apply=%region_1.0 | all-reduce | flops 32 | bytes 256 | tf_op jit(solution)/shard_map/psum | solution.py:35
  49.5 35.0 %psum.22 = f32[32]{0:T(128)S(1)} all-reduce(f32[32]{0:T(128)S(1)} %psum.21), channel_id=1, replica_groups=mesh['row'=8,'col'=8,'tm'=8] {'col'}, use_global_device_ids=true, to_apply=%region_2.0 | all-reduce | flops 32 | bytes 256 | tf_op jit(solution)/shard_map/psum | solution.py:35
  84.5 0.0 copy-done.1
  84.5 0.2 fusion
  84.7 26.5 %psum.23 = f32[3,1000]{1,0:T(4,128)} all-reduce(f32[3,1000]{1,0:T(4,128)S(1)} %fusion), channel_id=1, replica_groups=mesh['row'=8,'col'=8,'tm'=8] {'row'}, use_global_device_ids=true, to_apply=%region_3.0 | all-reduce | flops 3000 | bytes 24000 | tf_op jit(solution)/shard_map/psum | solution.py:42
  (2 shorter events, 0.0 us)
Async XLA Ops:
  5.9 22.9 %all-to-all-start = ((bf16[8,2,15360]{2,1,0:T(2,128)(2,1)}), bf16[8,2,15360]{2,1,0:T(2,128)(2,1)S(1)}, u32[]{:S(2)}, u32[]{:S(2)}) async-start(bf16[8,2,15360]{2,1,0:T(2,128)(2,1)} %reshape.19), calls=%async_computation | async-start | bytes 983040 | tf_op jit(solution)/shard_map/all_to_all | solution.py:27
  29.7 2.0 %copy-start = (bf16[16,32,480]{2,1,0:T(8,128)(2,1)S(1)}, bf16[16,32,480]{2,1,0:T(8,128)(2,1)}, u32[]{:S(2)}) copy-start(bf16[16,32,480]{2,1,0:T(8,128)(2,1)} %param.8) | copy-start | bytes 1474564
  31.3 53.3 %copy-start.1 = (f32[3,32]{1,0:T(4,128)S(1)}, f32[3,32]{1,0:T(4,128)}, u32[]{:S(2)}) copy-start(f32[3,32]{1,0:T(4,128)} %param.9) | copy-start | bytes 1156
